TPU v7x, 128 devices: a whole 4x4x4 slice. The times are simulated.
128 devices in a mesh: dp: 4 (over z_lo, core), mp: 32 (over y, z_hi, x).
Axes of the slice: x: 4, y: 4, z: 4 (z_hi: 2, z_lo: 2; z = z_hi * 2 + z_lo), core: 2. Of those that a mesh axis runs over, the one named last changes fastest.
Arguments:
- fields: float32 [4, 32, 128, 128, 128], P('dp', None, 'mp'), may hold values from -6 to 6
- upstream: bfloat16 [4, 32, 128, 128, 128], P('dp', None, 'mp'), may hold values from -6 to 6
- spectral_weight: float32 [2, 32, 32, 32, 1024], P(None, None, None, 'dp', 'mp'), may hold values from -4.2 to 4.2
- point_weight: float32 [32, 32], replicated, may hold values from -1 to 1
- point_bias: float32 [32], replicated, may hold values from -3 to 3
Outputs:
- grad_fields: float32 [4, 32, 128, 128, 128], P('dp', None, 'mp')
- grad_weight: float32 [2, 32, 32, 32, 1024], P(None, None, None, 'dp', 'mp')
All inputs are finite; a program needn't handle non-finite values.
Results may differ from a plain program's by a relative error of at most 0.0003.
Values sent between devices are 32-bit elements; how exact they have to be, the bound alone decides.
A program may use at most 256 MiB of HBM per device.

v0:
```python
from functools import partial
import math
import jax
import jax.numpy as jnp
from jax import lax
from jax.sharding import PartitionSpec as P

NX = 128
NY = 128
NZ = 128
MX = 32
MY = 32
MZ = 32
HIGHEST = lax.Precision.HIGHEST


def tables(number, kept_modes, signed):
    positions = jnp.arange(number, dtype=jnp.int32)
    frequency = jnp.arange(kept_modes, dtype=jnp.int32)
    if signed:
        frequency = jnp.where(frequency < kept_modes // 2, frequency, frequency - kept_modes)
    phases = jnp.mod(positions[:, None] * frequency[None, :], number).astype(jnp.float32) * (
        2.0 * math.pi / number
    )
    return jnp.concatenate([jnp.cos(phases), jnp.sin(phases)], axis=1)


def forward_plane(grid_field, table_y, table_z):
    along_y = jnp.einsum("scpyz,yj->scpjz", grid_field, table_y, precision=HIGHEST)
    products = jnp.einsum("scpjz,zk->scpjk", along_y, table_z, precision=HIGHEST)
    cos_cos = products[:, :, :, :MY, :MZ]
    cos_sin = products[:, :, :, :MY, MZ:]
    sin_cos = products[:, :, :, MY:, :MZ]
    sin_sin = products[:, :, :, MY:, MZ:]
    result = jnp.stack([cos_cos - sin_sin, -(sin_cos + cos_sin)], axis=3)
    return result.reshape(result.shape[:4] + (MY * MZ,))


def forward_line(pieces, table_x):
    products = jnp.einsum("scxrm,xk->scrkm", pieces, table_x, precision=HIGHEST)
    real_part = products[:, :, 0, :MX] + products[:, :, 1, MX:]
    imag_part = products[:, :, 1, :MX] - products[:, :, 0, MX:]
    return jnp.stack([real_part, imag_part], axis=2)


def inverse_line(spectrum, table_x):
    real_part = spectrum[:, :, 0]
    imag_part = spectrum[:, :, 1]
    stacked = jnp.stack(
        [
            jnp.concatenate([real_part, -imag_part], axis=2),
            jnp.concatenate([imag_part, real_part], axis=2),
        ],
        axis=2,
    )
    return jnp.einsum("scrjm,xj->scxrm", stacked, table_x, precision=HIGHEST)


def inverse_plane(pieces, table_y, table_z):
    shaped = pieces.reshape(pieces.shape[:4] + (MY, MZ))
    real_part = shaped[:, :, :, 0]
    imag_part = shaped[:, :, :, 1]
    stacked = jnp.stack(
        [
            jnp.concatenate([real_part, -imag_part], axis=3),
            jnp.concatenate([imag_part, real_part], axis=3),
        ],
        axis=3,
    )
    along_y = jnp.einsum("scpwjk,yj->scpwyk", stacked, table_y, precision=HIGHEST)
    merged = jnp.concatenate([along_y[:, :, :, 0], -along_y[:, :, :, 1]], axis=4)
    return jnp.einsum("scpyj,zj->scpyz", merged, table_z, precision=HIGHEST)


def mix_forward(weight, spectrum):
    real_weight = weight[0]
    imag_weight = weight[1]
    real_spec = spectrum[:, :, 0]
    imag_spec = spectrum[:, :, 1]
    real_part = jnp.einsum(
        "sixm,ioxm->soxm", real_spec, real_weight, precision=HIGHEST
    ) - jnp.einsum("sixm,ioxm->soxm", imag_spec, imag_weight, precision=HIGHEST)
    imag_part = jnp.einsum(
        "sixm,ioxm->soxm", imag_spec, real_weight, precision=HIGHEST
    ) + jnp.einsum("sixm,ioxm->soxm", real_spec, imag_weight, precision=HIGHEST)
    return jnp.stack([real_part, imag_part], axis=2)


def mix_adjoint(weight, gradient):
    real_weight = weight[0]
    imag_weight = weight[1]
    real_grad = gradient[:, :, 0]
    imag_grad = gradient[:, :, 1]
    real_part = jnp.einsum(
        "soxm,ioxm->sixm", real_grad, real_weight, precision=HIGHEST
    ) + jnp.einsum("soxm,ioxm->sixm", imag_grad, imag_weight, precision=HIGHEST)
    imag_part = jnp.einsum(
        "soxm,ioxm->sixm", imag_grad, real_weight, precision=HIGHEST
    ) - jnp.einsum("soxm,ioxm->sixm", real_grad, imag_weight, precision=HIGHEST)
    return jnp.stack([real_part, imag_part], axis=2)


def weight_gradient(gradient, spectrum):
    real_grad = gradient[:, :, 0]
    imag_grad = gradient[:, :, 1]
    real_spec = spectrum[:, :, 0]
    imag_spec = spectrum[:, :, 1]
    real_part = jnp.einsum("soxm,sixm->ioxm", real_grad, real_spec, precision=HIGHEST) + jnp.einsum(
        "soxm,sixm->ioxm", imag_grad, imag_spec, precision=HIGHEST
    )
    imag_part = jnp.einsum("soxm,sixm->ioxm", imag_grad, real_spec, precision=HIGHEST) - jnp.einsum(
        "soxm,sixm->ioxm", real_grad, imag_spec, precision=HIGHEST
    )
    return jnp.stack([real_part, imag_part], axis=0)


def shards(fields, upstream, spectral_weight, point_weight, point_bias):
    table_y = tables(NY, MY, True)
    table_z = tables(NZ, MZ, False)
    table_x = tables(NX, MX, True)
    modes_dev = spectral_weight.shape[4]
    mode_index = lax.axis_index("mp") * modes_dev + jnp.arange(modes_dev, dtype=jnp.int32)
    kz_index = jnp.mod(mode_index, MZ)
    factor = jnp.where(kz_index == 0, 1.0, 2.0).astype(jnp.float32) / float(NX * NY * NZ)

    def to_modes(pieces):
        return forward_line(pieces, table_x)

    def to_cells(pieces):
        return inverse_plane(pieces, table_y, table_z)

    spectrum = to_modes(
        lax.all_to_all(
            forward_plane(fields, table_y, table_z), "mp", split_axis=4, concat_axis=2, tiled=True
        )
    )
    full_weight = lax.all_gather(spectral_weight, "dp", axis=3, tiled=True)
    mixed_spec = mix_forward(full_weight, spectrum)
    mixed_spec = mixed_spec * factor
    spectral_part = to_cells(
        lax.all_to_all(
            inverse_line(mixed_spec, table_x), "mp", split_axis=2, concat_axis=4, tiled=True
        )
    )
    preact = spectral_part + jnp.einsum("scpyz,co->sopyz", fields, point_weight, precision=HIGHEST)
    preact = preact + point_bias[None, :, None, None, None]
    activation, pullback = jax.vjp(partial(jax.nn.gelu, approximate=False), preact)
    grad_pre = pullback(upstream.astype(jnp.float32))[0]
    grad_spec = to_modes(
        lax.all_to_all(
            forward_plane(grad_pre, table_y, table_z), "mp", split_axis=4, concat_axis=2, tiled=True
        )
    )
    grad_spec = grad_spec * factor
    back_spec = mix_adjoint(full_weight, grad_spec)
    weight_out = lax.psum_scatter(
        weight_gradient(grad_spec, spectrum), "dp", scatter_dimension=3, tiled=True
    )
    spectral_back = to_cells(
        lax.all_to_all(
            inverse_line(back_spec, table_x), "mp", split_axis=2, concat_axis=4, tiled=True
        )
    )
    grad_fields = spectral_back + jnp.einsum(
        "sopyz,co->scpyz", grad_pre, point_weight, precision=HIGHEST
    )
    return (grad_fields, weight_out)


def solution(mesh):
    placed = (
        P("dp", None, "mp", None, None),
        P("dp", None, "mp", None, None),
        P(None, None, None, "dp", "mp"),
        P(),
        P(),
    )
    return jax.shard_map(
        shards,
        mesh=mesh,
        in_specs=placed,
        out_specs=(P("dp", None, "mp", None, None), P(None, None, None, "dp", "mp")),
        check_vma=False,
    )
```

profile of v0, /device:TPU:1, one launch (start us, length us, event | category | flops | bytes accessed | tf_op | source)
XLA Modules:
  0.0 849.2 jit_solution(7774384556777394916)
XLA Ops:
  8.2 6.8 fusion.70
  15.0 3.6 fusion.46
  18.6 2.5 slice_subtract_fusion.1
  21.1 3.6 copy.236
  24.7 2.5 copy.237
  27.2 9.9 %fusion.108 = f32[1024,1,4,2,32]{4,3,2,1,0:T(2,128)} fusion(f32[1,32,4,1,1024]{1,3,2,0,4:T(1,128)} %bitcast.341, f32[1,32,4,1,1024]{1,3,2,0,4:T(1,128)} %bitcast.339), kind=kLoop, calls=%fused_computation.186 | loop fusion | flops 262144 | bytes 2097152
  37.1 6.7 reshape.415
  43.8 11.3 %all-to-all-start = ((f32[32,1,8192]{2,1,0:T(1,128)}), f32[32,1,8192]{2,1,0:T(1,128)S(1)}, u32[]{:S(2)}, u32[]{:S(2)}) async-start(f32[32,1,8192]{2,1,0:T(1,128)} %reshape.415), calls=%async_computation | async-start | bytes 2097152 | tf_op jit(solution)/shard_map/all_to_all | solution.py:133
  55.2 17.2 %all-to-all-done = f32[32,1,8192]{2,1,0:T(1,128)S(1)} async-done(((f32[32,1,8192]{2,1,0:T(1,128)}), f32[32,1,8192]{2,1,0:T(1,128)S(1)}, u32[]{:S(2)}, u32[]{:S(2)}) %all-to-all-start) | async-done | bytes 1048608 | tf_op jit(solution)/shard_map/all_to_all | solution.py:133
  72.9 3.3 reduce.16
  76.2 4.9 reshape.416
  81.0 7.4 copy.238
  88.4 6.6 copy.146
  95.1 3.8 copy.147
  98.8 1.0 fusion.102
  100.5 214.9 %all-gather.2.cloned.1.call-done = f32[2,32,32,32,32]{4,3,2,1,0:T(8,128)} async-done(((f32[2,32,32,8,32]{4,3,2,1,0:T(8,128)}), f32[2,32,32,32,32]{4,3,2,1,0:T(8,128)}) %all-gather.2.cloned.1.call-update) | async-done | bytes 8388624 | tf_op jit(solution)/shard_map/all_gather | solution.py:137
  315.5 13.5 %fusion.4 = (f32[32,32,32]{1,0,2:T(8,128)S(1)}, f32[32,32,32]{1,0,2:T(8,128)S(1)}, f32[32,32,32]{1,0,2:T(8,128)S(1)}, f32[32,32,32]{1,0,2:T(8,128)S(1)}) fusion(f32[2,32,32,32,32]{4,3,2,1,0:T(8,128)} %all-gather.2.cloned.1.call-done, f32[32,32,32]{1,0,2:T(8,128)S(1)} %copy.250, f32[32,32,32]{1,0,2:T(8,128)S(1)} %copy.249), kind=kLoop, calls=%fused_computation.11 | loop fusion | flops 8257536 | bytes 9175040
  329.0 1.0 copy.190
  330.7 1.1 subtract_bitcast_fusion.2
  333.5 4.3 copy.149
  337.8 6.5 reshape.417
  344.3 9.1 %all-to-all-start.1 = ((f32[32,1,8192]{2,1,0:T(1,128)}), f32[32,1,8192]{2,1,0:T(1,128)S(1)}, u32[]{:S(2)}, u32[]{:S(2)}) async-start(f32[32,1,8192]{2,1,0:T(1,128)} %reshape.417), calls=%async_computation.1 | async-start | bytes 2097152 | tf_op jit(solution)/shard_map/all_to_all | solution.py:141
  353.5 16.3 %fusion.21 = f32[32,4,128,128]{3,0,2,1:T(8,128)} fusion(f32[32,4,128,128]{3,2,1,0:T(8,128)} %bitcast.318, f32[32,32]{1,0:T(8,128)S(1)} %copy-done), kind=kOutput, calls=%fused_computation.37 | convolution fusion | flops 805306368 | bytes 16781312 | tf_op jit(solution)/shard_map/scpyz,co->sopyz/dot_general | solution.py:145
  369.8 1.5 all-to-all-done.1
  371.3 3.3 reduce.17
  374.6 4.9 reshape.418
  379.5 7.9 copy.151
  387.4 1.8 fusion.104
  389.2 2.7 slice_bitcast_fusion.4
  391.9 1.1 maximum_bitcast_fusion.16
  393.1 3.4 fusion.53
  397.7 44.8 %fusion.13 = f32[32,4,128,128]{3,2,1,0:T(8,128)S(1)} fusion(bf16[1,32,4,128,128]{4,3,2,1,0:T(8,128)(2,1)S(1)} %copy-done.2, f32[32,4,128,128]{3,0,2,1:T(8,128)S(1)} %bitcast.338, f32[32]{0:T(128)S(1)} %copy-done.3, f32[1,32,4,128,32]{3,4,2,1,0:T(8,128)S(1)} %get-tuple-element.23, f32[1,32,4,128,32]{3,4,2,1,0:T(8,128)S(1)} %get-tuple-element.22, ...), kind=kOutput, calls=%fused_computation.27 | convolution fusion | flops 1766858752 | bytes 25198720 | tf_op jit(solution)/shard_map/scpyj,zj->scpyz/dot_general | solution.py:72
  442.6 3.4 copy-done.1
  446.0 5.3 fusion.67
  451.3 3.6 fusion.49
  455.0 2.5 slice_subtract_fusion
  457.4 3.4 copy.242
  460.8 2.4 copy.243
  463.3 8.9 %fusion.107 = f32[1024,1,4,2,32]{4,3,2,1,0:T(2,128)} fusion(f32[1,32,4,1,1024]{1,3,2,0,4:T(1,128)} %bitcast.342, f32[1,32,4,1,1024]{1,3,2,0,4:T(1,128)} %bitcast.340), kind=kLoop, calls=%fused_computation.185 | loop fusion | flops 262144 | bytes 2097152
  472.2 5.8 reshape.419
  478.0 26.0 %all_to_all.60 = f32[32,1,8192]{2,1,0:T(1,128)S(1)} all-to-all(f32[32,1,8192]{2,1,0:T(1,128)S(1)} %reshape.419), channel_id=1, replica_groups=mesh['dp'=4,'mp'=32] {'mp'}, dimensions={0} | all-to-all | bytes 2097152 | tf_op jit(solution)/shard_map/all_to_all | solution.py:150
  503.9 3.3 reduce.18
  507.2 4.9 reshape.420
  512.1 7.5 copy.244
  519.6 6.6 copy.160
  526.2 3.8 copy.161
  532.1 5.8 add_bitcast_fusion
  537.9 14.0 %pad_maximum_fusion = f32[2,32,32,32,32]{4,3,2,1,0:T(8,128)} fusion(f32[1,32,32,32,32]{4,3,2,1,0:T(8,128)S(1)} %get-tuple-element.29, f32[1,32,32,32,32]{4,3,2,1,0:T(8,128)S(1)} %get-tuple-element.28), kind=kLoop, calls=%fused_computation | loop fusion | flops 2097152 | bytes 16777216 | tf_op jit(solution)/shard_map/stack | solution.py:114
  552.0 15.6 %fusion.1 = (f32[32,32,32]{1,0,2:T(8,128)S(1)}, f32[32,32,32]{1,0,2:T(8,128)S(1)}, f32[32,32,32]{1,0,2:T(8,128)S(1)}, f32[32,32,32]{1,0,2:T(8,128)S(1)}) fusion(f32[2,32,32,32,32]{4,3,2,1,0:T(8,128)} %all-gather.2.cloned.1.call-done, f32[32,32,32]{1,0,2:T(8,128)S(1)} %copy.251, f32[32,32,32]{1,0,2:T(8,128)S(1)} %copy.252), kind=kLoop, calls=%fused_computation.4 | loop fusion | flops 8257536 | bytes 9175040
  567.6 1.0 copy.234
  569.2 1.2 fusion.106
  571.7 4.5 copy.164
  576.3 6.5 reshape.421
  582.8 5.6 all-to-all-start.3
  588.4 17.7 %fusion.18 = f32[4,128,128,32]{2,3,1,0:T(8,128)} fusion(f32[32,4,128,128]{3,2,1,0:T(8,128)} %copy-done.1, f32[32,32]{1,0:T(8,128)S(1)} %copy-done), kind=kOutput, calls=%fused_computation.33 | convolution fusion | flops 805306368 | bytes 16781312 | tf_op jit(solution)/shard_map/sopyz,co->scpyz/dot_general | solution.py:164
  606.1 3.3 reduce.19
  609.4 4.9 reshape.422
  614.3 7.8 copy.166
  622.1 1.8 fusion.105
  624.0 2.7 slice_bitcast_fusion.1
  626.7 1.2 maximum_bitcast_fusion.18
  627.8 3.4 fusion.52
  631.8 22.5 %fusion.17 = f32[1,32,4,128,128]{4,3,2,1,0:T(8,128)} fusion(f32[4,128,128,32]{2,3,1,0:T(8,128)S(1)} %bitcast.320, f32[1,32,4,128,32]{3,4,2,1,0:T(8,128)S(1)} %get-tuple-element.17, f32[1,32,4,128,32]{3,4,2,1,0:T(8,128)S(1)} %get-tuple-element.16, f32[128,32]{0,1:T(8,128)S(1)} %get-tuple-element.48, f32[128,32]{0,1:T(8,128)S(1)} %get-tuple-element.49), kind=kOutput, calls=%fused_computation.32 | convolution fusion | flops 1613766656 | bytes 21004288 | tf_op jit(solution)/shard_map/scpyj,zj->scpyz/dot_general | solution.py:72
  654.3 187.8 %reduce-scatter.2.cloned.1.call-done = f32[2,32,32,8,32]{4,3,2,1,0:T(8,128)} async-done(((f32[2,32,32,32,32]{4,3,2,1,0:T(8,128)}), f32[2,32,32,8,32]{4,3,2,1,0:T(8,128)}) %reduce-scatter.2.cloned.1.call-update) | async-done | bytes 2097168 | tf_op jit(solution)/shard_map/reduce_scatter | solution.py:156
  (54 shorter events, 10.5 us)
Async XLA Ops:
  7.2 346.3 %copy-start = (f32[32,32]{1,0:T(8,128)S(1)}, f32[32,32]{1,0:T(8,128)}, u32[]{:S(2)}) copy-start(f32[32,32]{1,0:T(8,128)} %param.8) | copy-start | bytes 12292
  7.2 308.3 %all-gather.2.cloned.1.call-start = ((), (), s32[]{:S(2)}) async-start(), calls=%async_computation.5 | async-start | bytes 41943040 | tf_op jit(solution)/shard_map/all_gather | solution.py:137
  43.8 28.5 %all-to-all-start = ((f32[32,1,8192]{2,1,0:T(1,128)}), f32[32,1,8192]{2,1,0:T(1,128)S(1)}, u32[]{:S(2)}, u32[]{:S(2)}) async-start(f32[32,1,8192]{2,1,0:T(1,128)} %reshape.415), calls=%async_computation | async-start | bytes 2097152 | tf_op jit(solution)/shard_map/all_to_all | solution.py:133
  344.3 27.0 %all-to-all-start.1 = ((f32[32,1,8192]{2,1,0:T(1,128)}), f32[32,1,8192]{2,1,0:T(1,128)S(1)}, u32[]{:S(2)}, u32[]{:S(2)}) async-start(f32[32,1,8192]{2,1,0:T(1,128)} %reshape.417), calls=%async_computation.1 | async-start | bytes 2097152 | tf_op jit(solution)/shard_map/all_to_all | solution.py:141
  353.4 488.6 %reduce-scatter.2.cloned.1.call-start = ((), (), s32[]{:S(2)}) async-start(), calls=%async_computation.6 | async-start | bytes 41943040 | tf_op jit(solution)/shard_map/reduce_scatter | solution.py:156
  393.1 4.2 slice-start.2
  393.1 4.2 slice-start.3
  393.1 4.6 copy-start.2
  393.1 4.6 copy-start.3
  442.6 3.4 copy-start.1
  582.8 23.4 %all-to-all-start.3 = ((f32[32,1,8192]{2,1,0:T(1,128)}), f32[32,1,8192]{2,1,0:T(1,128)S(1)}, u32[]{:S(2)}, u32[]{:S(2)}) async-start(f32[32,1,8192]{2,1,0:T(1,128)} %reshape.421), calls=%async_computation.3 | async-start | bytes 2097152 | tf_op jit(solution)/shard_map/all_to_all | solution.py:160
  627.8 3.9 slice-start
  627.8 3.9 slice-start.1
Sparse Core Ops, SparseCore 0:
  9.7 305.7 all-gather.1
  552.1 289.8 reduce-scatter.1
where the time goes:
time: 857 us; the launch traced here: 849 us
  waiting for transfers between devices  422 us (49%)
  local copies, waits for them, and re-layouts  131 us (15%)
  matrix products  131 us (15%)
  other arithmetic  97.4 us (11%)
  starting transfers between devices  26.2 us (3%)
  blocking collectives  26 us (3%)
  between operations  15 us (2%)
    all_gather x1, waiting for transfers between devices, shards(): full_weight = lax.all_gather(spectral_weight, 'dp', axis=3, tiled=True)  215 us
    reduce_scatter x1, waiting for transfers between devices, shards(): lax.psum_scatter(weight_gradient(grad_spec, spectrum), 'dp', scatter_dime...  188 us
    dot_general x2, matrix products, inverse_plane(): return jnp.einsum('scpyj,zj->scpyz', merged, table_z, precision=HIGHEST)  67.3 us
    unnamed x29, local copies, waits for them, and re-layouts  49.8 us
    unnamed x7, other arithmetic  48.2 us
    all_to_all x1, blocking collectives, shards(): lax.all_to_all(forward_plane(grad_pre, table_y, table_z), 'mp', split_axi...  26 us
    another operation x2, other arithmetic, weight_gradient(): return jnp.stack([real_part, imag_part], axis=0)  19.8 us
    dot_general x1, matrix products, shards(): jnp.einsum('sopyz,co->scpyz', grad_pre, point_weight, precision=HIGHEST)  17.7 us
  transfers between devices with their start and end apart: 5, of which 4 were waited for; matrix products, arithmetic and copies ran while one was open for 21% of the time, Pallas kernels for 0%

commit v1 on v0

--- a/solution.py
+++ b/solution.py
@@ -12,6 +12,11 @@
 MY = 32
 MZ = 32
 HIGHEST = lax.Precision.HIGHEST
+
+
+def swapped_in(block, axis, dim):
+    sent = jnp.stack([block] * lax.axis_size(axis))
+    return jnp.concatenate(lax.all_to_all(sent, axis, 0, 0), axis=dim)
 
 
 def tables(number, kept_modes, signed):
@@ -134,7 +139,7 @@
             forward_plane(fields, table_y, table_z), "mp", split_axis=4, concat_axis=2, tiled=True
         )
     )
-    full_weight = lax.all_gather(spectral_weight, "dp", axis=3, tiled=True)
+    full_weight = swapped_in(spectral_weight, "dp", 3)
     mixed_spec = mix_forward(full_weight, spectrum)
     mixed_spec = mixed_spec * factor
     spectral_part = to_cells(

time: 857 us -> 820 us (0.957)
  waiting for transfers between devices: 422 us -> 254 us
  local copies, waits for them, and re-layouts: 131 us -> 232 us
  other arithmetic: 97.4 us -> 125 us
    all_gather x1 -> x0, waiting for transfers between devices: 215 us -> none  [shards(): full_weight = lax.all_gather(spectral_weight, 'dp', axis=3, tiled=True)]
    unnamed x29 -> x31, local copies, waits for them, and re-layouts: 49.8 us -> 114 us
    all_to_all x0 -> x1, waiting for transfers between devices: none -> 64.2 us  [swapped_in(): return jnp.concatenate(lax.all_to_all(sent, axis, 0, 0), axis=dim)]
    all_to_all x0 -> x1, other arithmetic: none -> 28.5 us  [swapped_in(): return jnp.concatenate(lax.all_to_all(sent, axis, 0, 0), axis=dim)]
    all_to_all x0 -> x2, local copies, waits for them, and re-layouts: none -> 23.8 us  [swapped_in(): return jnp.concatenate(lax.all_to_all(sent, axis, 0, 0), axis=dim)]
    all_to_all x1, waiting for transfers between devices: 17.2 us -> 0.01 us  [shards(): lax.all_to_all(forward_plane(fields, table_y, table_z), 'mp', split_axis=...]
    another operation x2 -> x3, local copies, waits for them, and re-layouts: 7.51 us -> 21.5 us  [the longest x1 13.9 us: swapped_in(): sent = jnp.stack([block] * lax.axis_size(axis))]
  transfers between devices with their start and end apart: 5 -> 5, of which waited for: 4 -> 3; matrix products, arithmetic and copies ran while one was open for 21% -> 23% of each run, Pallas kernels for 0% -> 0%
where the time goes in v1:
time: 820 us; the launch traced here: 812 us
  waiting for transfers between devices  254 us (31%)
  local copies, waits for them, and re-layouts  232 us (28%)
  matrix products  128 us (16%)
  other arithmetic  125 us (15%)
  starting transfers between devices  33 us (4%)
  blocking collectives  25.2 us (3%)
  between operations  15 us (2%)
    reduce_scatter x1, waiting for transfers between devices, shards(): lax.psum_scatter(weight_gradient(grad_spec, spectrum), 'dp', scatter_dime...  190 us
    unnamed x31, local copies, waits for them, and re-layouts  114 us
    all_to_all x1, waiting for transfers between devices, swapped_in(): return jnp.concatenate(lax.all_to_all(sent, axis, 0, 0), axis=dim)  64.2 us
    dot_general x2, matrix products, inverse_plane(): return jnp.einsum('scpyj,zj->scpyz', merged, table_z, precision=HIGHEST)  63.7 us
    unnamed x7, other arithmetic  47.3 us
    all_to_all x1, other arithmetic, swapped_in(): return jnp.concatenate(lax.all_to_all(sent, axis, 0, 0), axis=dim)  28.5 us
    all_to_all x1, blocking collectives, shards(): lax.all_to_all(forward_plane(grad_pre, table_y, table_z), 'mp', split_axi...  25.2 us
    all_to_all x2, local copies, waits for them, and re-layouts, swapped_in(): return jnp.concatenate(lax.all_to_all(sent, axis, 0, 0), axis=dim)  23.8 us
  transfers between devices with their start and end apart: 5, of which 3 were waited for; matrix products, arithmetic and copies ran while one was open for 23% of the time, Pallas kernels for 0%

profile of v1, /device:TPU:1, one launch (start us, length us, event | category | flops | bytes accessed | tf_op | source)
XLA Modules:
  0.0 812.1 jit_solution(4878672367859265267)
XLA Ops:
  7.4 6.8 fusion.70
  14.2 3.6 fusion.46
  17.9 2.5 slice_subtract_fusion.1
  20.3 3.3 copy.240
  23.7 2.5 copy.239
  26.2 8.9 %fusion.108 = f32[1024,1,4,2,32]{4,3,2,1,0:T(2,128)} fusion(f32[1,32,4,1,1024]{1,3,2,0,4:T(1,128)} %bitcast.344, f32[1,32,4,1,1024]{1,3,2,0,4:T(1,128)} %bitcast.346), kind=kLoop, calls=%fused_computation.187 | loop fusion | flops 262144 | bytes 2097152
  35.1 6.5 reshape.428
  41.6 11.2 %all-to-all-start = ((f32[32,1,8192]{2,1,0:T(1,128)}), f32[32,1,8192]{2,1,0:T(1,128)S(1)}, u32[]{:S(2)}, u32[]{:S(2)}) async-start(f32[32,1,8192]{2,1,0:T(1,128)} %reshape.428), calls=%async_computation | async-start | bytes 2097152 | tf_op jit(solution)/shard_map/all_to_all | solution.py:138
  52.8 13.9 %stack.87 = f32[4,2,32,32,8,32]{5,4,3,2,1,0:T(8,128)} broadcast(f32[2,32,32,8,32]{4,3,2,1,0:T(8,128)} %param.7), dimensions={1,2,3,4,5} | broadcast | bytes 10485760 | tf_op jit(solution)/shard_map/stack | solution.py:18
  66.7 33.4 %reshape.426 = f32[4,1,524288]{2,1,0:T(1,128)} reshape(f32[4,2,32,32,8,32]{5,4,3,2,1,0:T(8,128)} %stack.87) | data formatting | bytes 16777216
  100.2 7.0 all-to-all-start.1
  107.7 3.2 reduce.17
  110.9 4.9 reshape.429
  115.8 7.5 copy.241
  123.2 6.6 copy.148
  129.9 3.8 copy.149
  135.4 64.2 %all-to-all-done.1 = f32[4,1,524288]{2,1,0:T(1,128)} async-done(((f32[4,1,524288]{2,1,0:T(1,128)}), f32[4,1,524288]{2,1,0:T(1,128)}, u32[]{:S(2)}, u32[]{:S(2)}) %all-to-all-start.1) | async-done | bytes 8388640 | tf_op jit(solution)/shard_map/all_to_all | solution.py:19
  199.5 28.5 %reduce.16 = f32[4,524288]{1,0:T(4,128)} reduce(f32[4,1,524288]{2,1,0:T(1,128)} %all-to-all-done.1, f32[]{:T(128)} %broadcast.198), dimensions={1}, to_apply=%all_to_all.50.reduce_sub_computation | reduce | bytes 16777220 | tf_op jit(solution)/shard_map/all_to_all | solution.py:19
  228.1 31.1 %reshape.427 = f32[4,2,32,32,8,32]{5,4,3,2,1,0:T(8,128)} reshape(f32[4,524288]{1,0:T(4,128)} %reduce.16) | data formatting | bytes 16777216
  259.1 23.3 %copy.268 = f32[4,2,32,32,8,32]{5,4,0,3,2,1:T(8,128)} copy(f32[4,2,32,32,8,32]{5,4,3,2,1,0:T(8,128)} %reshape.427) | data formatting | bytes 16777216 | tf_op jit(solution)/shard_map/all_to_all | solution.py:19
  282.4 13.4 %fusion.4 = (f32[32,32,32]{1,0,2:T(8,128)S(1)}, f32[32,32,32]{1,0,2:T(8,128)S(1)}, f32[32,32,32]{1,0,2:T(8,128)S(1)}, f32[32,32,32]{1,0,2:T(8,128)S(1)}) fusion(f32[2,32,32,4,8,32]{5,4,3,2,1,0:T(8,128)} %bitcast.321, f32[32,32,32]{1,0,2:T(8,128)S(1)} %copy.253, f32[32,32,32]{1,0,2:T(8,128)S(1)} %copy.252), kind=kLoop, calls=%fused_computation.12 | loop fusion | flops 8257536 | bytes 9175040
  300.3 4.3 copy.152
  304.6 6.5 reshape.430
  311.1 9.5 %all-to-all-start.2 = ((f32[32,1,8192]{2,1,0:T(1,128)}), f32[32,1,8192]{2,1,0:T(1,128)S(1)}, u32[]{:S(2)}, u32[]{:S(2)}) async-start(f32[32,1,8192]{2,1,0:T(1,128)} %reshape.430), calls=%async_computation.2 | async-start | bytes 2097152 | tf_op jit(solution)/shard_map/all_to_all | solution.py:146
  320.7 16.5 %fusion.21 = f32[32,4,128,128]{3,0,2,1:T(8,128)} fusion(f32[32,4,128,128]{3,2,1,0:T(8,128)} %bitcast.323, f32[32,32]{1,0:T(8,128)S(1)} %copy-done), kind=kOutput, calls=%fused_computation.38 | convolution fusion | flops 805306368 | bytes 16781312 | tf_op jit(solution)/shard_map/scpyz,co->sopyz/dot_general | solution.py:150
  337.4 3.2 reduce.18
  340.6 4.9 reshape.431
  345.4 7.6 copy.154
  353.0 1.8 fusion.104
  354.8 2.7 slice_bitcast_fusion.4
  357.5 1.1 maximum_bitcast_fusion.16
  358.7 3.4 fusion.53
  363.3 41.2 %fusion.13 = f32[32,4,128,128]{3,2,1,0:T(8,128)S(1)} fusion(bf16[1,32,4,128,128]{4,3,2,1,0:T(8,128)(2,1)S(1)} %copy-done.2, f32[32,4,128,128]{3,0,2,1:T(8,128)S(1)} %bitcast.343, f32[32]{0:T(128)S(1)} %copy-done.3, f32[1,32,4,128,32]{3,4,2,1,0:T(8,128)S(1)} %get-tuple-element.23, f32[1,32,4,128,32]{3,4,2,1,0:T(8,128)S(1)} %get-tuple-element.22, ...), kind=kOutput, calls=%fused_computation.28 | convolution fusion | flops 1766858752 | bytes 25198720 | tf_op jit(solution)/shard_map/scpyj,zj->scpyz/dot_general | solution.py:77
  404.5 3.4 copy-done.1
  407.9 5.3 fusion.67
  413.3 3.6 fusion.49
  416.9 2.5 slice_subtract_fusion
  419.4 3.4 copy.246
  422.8 2.4 copy.245
  425.2 8.9 %fusion.107 = f32[1024,1,4,2,32]{4,3,2,1,0:T(2,128)} fusion(f32[1,32,4,1,1024]{1,3,2,0,4:T(1,128)} %bitcast.345, f32[1,32,4,1,1024]{1,3,2,0,4:T(1,128)} %bitcast.347), kind=kLoop, calls=%fused_computation.186 | loop fusion | flops 262144 | bytes 2097152
  434.1 5.8 reshape.432
  439.9 25.2 %all_to_all.65 = f32[32,1,8192]{2,1,0:T(1,128)S(1)} all-to-all(f32[32,1,8192]{2,1,0:T(1,128)S(1)} %reshape.432), channel_id=1, replica_groups=mesh['dp'=4,'mp'=32] {'mp'}, dimensions={0} | all-to-all | bytes 2097152 | tf_op jit(solution)/shard_map/all_to_all | solution.py:155
  465.1 3.2 reduce.19
  468.3 4.9 reshape.433
  473.2 7.5 copy.247
  480.7 6.6 copy.163
  487.3 3.8 copy.164
  493.2 5.8 add_bitcast_fusion
  499.0 14.1 %pad_maximum_fusion = f32[2,32,32,32,32]{4,3,2,1,0:T(8,128)} fusion(f32[1,32,32,32,32]{4,3,2,1,0:T(8,128)S(1)} %get-tuple-element.29, f32[1,32,32,32,32]{4,3,2,1,0:T(8,128)S(1)} %get-tuple-element.28), kind=kLoop, calls=%fused_computation | loop fusion | flops 2097152 | bytes 16777216 | tf_op jit(solution)/shard_map/stack | solution.py:119
  513.1 15.8 %fusion.1 = (f32[32,32,32]{1,0,2:T(8,128)S(1)}, f32[32,32,32]{1,0,2:T(8,128)S(1)}, f32[32,32,32]{1,0,2:T(8,128)S(1)}, f32[32,32,32]{1,0,2:T(8,128)S(1)}) fusion(f32[2,32,32,4,8,32]{5,4,3,2,1,0:T(8,128)} %bitcast.322, f32[32,32,32]{1,0,2:T(8,128)S(1)} %copy.254, f32[32,32,32]{1,0,2:T(8,128)S(1)} %copy.255), kind=kLoop, calls=%fused_computation.5 | loop fusion | flops 8257536 | bytes 9175040
  530.6 1.1 fusion.106
  533.1 4.5 copy.167
  537.6 6.5 reshape.434
  544.2 5.2 all-to-all-start.4
  549.4 17.5 %fusion.18 = f32[4,128,128,32]{2,3,1,0:T(8,128)} fusion(f32[32,4,128,128]{3,2,1,0:T(8,128)} %copy-done.1, f32[32,32]{1,0:T(8,128)S(1)} %copy-done), kind=kOutput, calls=%fused_computation.34 | convolution fusion | flops 805306368 | bytes 16781312 | tf_op jit(solution)/shard_map/sopyz,co->scpyz/dot_general | solution.py:169
  566.9 3.2 reduce.20
  570.1 4.9 reshape.435
  574.9 7.8 copy.169
  582.8 1.9 fusion.105
  584.7 2.7 slice_bitcast_fusion.1
  587.4 1.2 maximum_bitcast_fusion.18
  588.6 3.4 fusion.52
  592.5 22.5 %fusion.17 = f32[1,32,4,128,128]{4,3,2,1,0:T(8,128)} fusion(f32[4,128,128,32]{2,3,1,0:T(8,128)S(1)} %bitcast.325, f32[1,32,4,128,32]{3,4,2,1,0:T(8,128)S(1)} %get-tuple-element.17, f32[1,32,4,128,32]{3,4,2,1,0:T(8,128)S(1)} %get-tuple-element.16, f32[128,32]{0,1:T(8,128)S(1)} %get-tuple-element.48, f32[128,32]{0,1:T(8,128)S(1)} %get-tuple-element.49), kind=kOutput, calls=%fused_computation.33 | convolution fusion | flops 1613766656 | bytes 21004288 | tf_op jit(solution)/shard_map/scpyj,zj->scpyz/dot_general | solution.py:77
  615.0 189.8 %reduce-scatter.2.cloned.1.call-done = f32[2,32,32,8,32]{4,3,2,1,0:T(8,128)} async-done(((f32[2,32,32,32,32]{4,3,2,1,0:T(8,128)}), f32[2,32,32,8,32]{4,3,2,1,0:T(8,128)}) %reduce-scatter.2.cloned.1.call-update) | async-done | bytes 2097168 | tf_op jit(solution)/shard_map/reduce_scatter | solution.py:161
  (58 shorter events, 14.0 us)
Async XLA Ops:
  7.2 313.5 %copy-start = (f32[32,32]{1,0:T(8,128)S(1)}, f32[32,32]{1,0:T(8,128)}, u32[]{:S(2)}) copy-start(f32[32,32]{1,0:T(8,128)} %param.8) | copy-start | bytes 12292
  41.6 58.6 %all-to-all-start = ((f32[32,1,8192]{2,1,0:T(1,128)}), f32[32,1,8192]{2,1,0:T(1,128)S(1)}, u32[]{:S(2)}, u32[]{:S(2)}) async-start(f32[32,1,8192]{2,1,0:T(1,128)} %reshape.428), calls=%async_computation | async-start | bytes 2097152 | tf_op jit(solution)/shard_map/all_to_all | solution.py:138
  100.2 99.4 %all-to-all-start.1 = ((f32[4,1,524288]{2,1,0:T(1,128)}), f32[4,1,524288]{2,1,0:T(1,128)}, u32[]{:S(2)}, u32[]{:S(2)}) async-start(f32[4,1,524288]{2,1,0:T(1,128)} %reshape.426), calls=%async_computation.1 | async-start | bytes 16777216 | tf_op jit(solution)/shard_map/all_to_all | solution.py:19
  311.1 26.3 %all-to-all-start.2 = ((f32[32,1,8192]{2,1,0:T(1,128)}), f32[32,1,8192]{2,1,0:T(1,128)S(1)}, u32[]{:S(2)}, u32[]{:S(2)}) async-start(f32[32,1,8192]{2,1,0:T(1,128)} %reshape.430), calls=%async_computation.2 | async-start | bytes 2097152 | tf_op jit(solution)/shard_map/all_to_all | solution.py:146
  320.7 484.2 %reduce-scatter.2.cloned.1.call-start = ((), (), s32[]{:S(2)}) async-start(), calls=%async_computation.6 | async-start | bytes 41943040 | tf_op jit(solution)/shard_map/reduce_scatter | solution.py:161
  358.7 4.2 slice-start.2
  358.7 4.2 slice-start.3
  358.7 4.6 copy-start.2
  358.7 4.6 copy-start.3
  404.5 3.4 copy-start.1
  544.2 22.7 %all-to-all-start.4 = ((f32[32,1,8192]{2,1,0:T(1,128)}), f32[32,1,8192]{2,1,0:T(1,128)S(1)}, u32[]{:S(2)}, u32[]{:S(2)}) async-start(f32[32,1,8192]{2,1,0:T(1,128)} %reshape.434), calls=%async_computation.4 | async-start | bytes 2097152 | tf_op jit(solution)/shard_map/all_to_all | solution.py:165
  588.6 3.9 slice-start
  588.6 3.9 slice-start.1
Sparse Core Ops, SparseCore 0:
  513.2 291.5 reduce-scatter.1
